TPU v7x, 32 devices: a whole 2x2x4 slice. The times are simulated.
32 devices in a mesh: wide: 8 (over y, x, core), quad: 4 (over z).
Axes of the slice: x: 2, y: 2, z: 4, core: 2. Of those that a mesh axis runs over, the one named last changes fastest.
Arguments:
- basis: float32 [16, 2097152], P(None, ('wide', 'quad')), may hold values from -6 to 6
- target: float32 [2097152], P(('wide', 'quad')), may hold values from -6 to 6
- sign_bits: int32 [2097152], P(('wide', 'quad')), may hold values from 0 to 1
- samples: int32 [8192], replicated, may hold values from 0 to 2097151
- owners: int32 [8192], replicated, may hold values from 0 to 7
Outputs:
- sketch: float32 [8192, 17], P(('wide', 'quad'))
- gram: float32 [8, 16, 17], P('quad')
Inputs may be any that keep to these rules, and one draw needn't show every extreme that they name: `samples`: sampled scenarios may repeat.
All inputs are finite; a program needn't handle non-finite values.
Results may differ from a plain program's by a relative error of at most 0.0003.
Values sent between devices are 32-bit elements; how exact they have to be, the bound alone decides.
A program may use at most 128 MiB of HBM per device.

v0:
```python
import math
import jax
import jax.numpy as jnp
from jax import lax
from jax.sharding import PartitionSpec as P

GROUPS = 8


def parity_sign(first, second, nbits):
    count = jnp.zeros_like(first)
    for bit in range(nbits):
        count = count + ((first & second) >> bit) & 1
    return (1 - 2 * (count & 1)).astype(jnp.float32)


def walsh_table(order):
    nbits = order.bit_length() - 1
    line = jnp.arange(order, dtype=jnp.int32)
    return parity_sign(line[:, None], line[None, :], nbits)


def shards(basis, target, sign_bits, samples, owners):
    rows = basis.shape[1]
    block = math.isqrt(rows)
    n_wide = lax.axis_size("wide")
    n_quad = lax.axis_size("quad")
    devices = n_wide * n_quad
    my_wide = lax.axis_index("wide")
    my_quad = lax.axis_index("quad")
    my_device = my_wide * n_quad + my_quad
    total_samples = samples.shape[0]
    per_dev = total_samples // devices
    scale = 1.0 / math.sqrt(rows * devices)
    flip = (1 - 2 * sign_bits).astype(jnp.float32)
    signed = jnp.concatenate([basis, target[None, :]], axis=0) * flip[None, :]
    width = signed.shape[0]
    table = walsh_table(block)
    cube = signed.reshape(width, block, block)
    cube = jnp.einsum("kab,ac->kcb", cube, table, precision=lax.Precision.HIGHEST)
    cube = jnp.einsum("kcb,bd->kcd", cube, table, precision=lax.Precision.HIGHEST)
    local = cube.reshape(width, rows)
    quarter = total_samples // n_quad
    quad_bits = n_quad.bit_length() - 1
    wide_bits = n_wide.bit_length() - 1
    line = jnp.arange(total_samples, dtype=jnp.int32)
    inner = line // quarter
    rest = line % quarter
    slots = (rest // per_dev * n_quad + inner) * per_dev + rest % per_dev
    number = samples[slots]
    values = jnp.take(local, number % rows, axis=1)
    source, values = (number // rows, values)
    sign = parity_sign(source % n_quad, jnp.full_like(source, my_quad), quad_bits)
    shared = lax.psum_scatter(values * sign[None, :], "quad", scatter_dimension=1, tiled=True)
    second = jnp.arange(quarter, dtype=jnp.int32)
    mine = (second // per_dev * n_quad + my_quad) * per_dev + second % per_dev
    outer = samples[mine] // rows // n_quad
    wide_sign = parity_sign(outer, jnp.full_like(outer, my_wide), wide_bits)
    columns = lax.psum_scatter(
        shared * (scale * wide_sign)[None, :], "wide", scatter_dimension=1, tiled=True
    )
    sketch = columns.T
    own_groups = lax.dynamic_slice_in_dim(owners, my_device * per_dev, per_dev, 0)
    onehot = (own_groups[:, None] == jnp.arange(GROUPS, dtype=jnp.int32)[None, :]).astype(
        jnp.float32
    )
    partial_gram = jnp.einsum(
        "rg,ri,rj->gij", onehot, sketch[:, : width - 1], sketch, precision=lax.Precision.HIGHEST
    )
    partial_gram = partial_gram * (GROUPS / total_samples)
    owned = GROUPS // n_quad
    summed = lax.psum(partial_gram, ("wide", "quad"))
    gram = lax.dynamic_slice_in_dim(summed, my_quad * owned, owned, 0)
    return (sketch, gram)


def solution(mesh):
    placed = (P(None, ("wide", "quad")), P(("wide", "quad")), P(("wide", "quad")), P(), P())
    return jax.shard_map(
        shards,
        mesh=mesh,
        in_specs=placed,
        out_specs=(P(("wide", "quad"), None), P("quad", None, None)),
        check_vma=False,
    )
```

profile of v0, /device:TPU:0, one launch (start us, length us, event | category | flops | bytes accessed | tf_op | source)
XLA Modules:
  0.0 308.2 jit_solution(10460242113116470487)
XLA Ops:
  7.2 0.0 copy-start
  7.2 0.0 reduce-scatter.3.cloned.1.call-start
  7.2 0.1 compare_select_fusion.1
  7.3 0.0 copy-start.1
  7.4 1.1 concatenate.9
  8.4 5.4 %copy.20 = f32[2,8,256,256]{3,2,1,0:T(8,128)} copy(f32[2,8,256,256]{3,1,2,0:T(8,128)} %bitcast.26) | data formatting | bytes 8388608
  13.8 0.0 copy-done.1
  13.8 0.1 mul.137
  13.9 6.7 %fusion = f32[256,17,256]{2,0,1:T(8,128)S(1)} fusion(f32[1,256,256]{2,1,0:T(8,128)S(1)} %concatenate.9, f32[16,256,256]{2,1,0:T(8,128)} %bitcast.25, f32[256,256]{1,0:T(8,128)S(1)} %mul.137), kind=kOutput, calls=%fused_computation.4 | convolution fusion | flops 3426615296 | bytes 9175040 | tf_op jit(solution)/shard_map/kab,ac->kcb/dot_general | solution.py:40
  20.6 5.7 %fusion.3 = f32[17,256,256]{2,1,0:T(8,128)} fusion(f32[256,17,256]{2,0,1:T(8,128)S(1)} %fusion), kind=kOutput, calls=%fused_computation.7 | convolution fusion | flops 3424387072 | bytes 8912896 | tf_op jit(solution)/shard_map/kcb,bd->kcd/dot_general | solution.py:41
  26.3 18.0 %copy.18 = f32[17,256,256]{0,2,1:T(8,128)} copy(f32[17,256,256]{2,1,0:T(8,128)} %fusion.3) | data formatting | bytes 8912896 | tf_op jit(solution)/shard_map/reshape | solution.py:42
  44.3 0.0 copy-done
  44.3 45.5 %gather_fusion = s32[8192]{0:T(1024)S(1)} fusion(s32[8192]{0:T(1024)S(1)} %copy-done, s32[8192]{0:T(1024)S(1)} %broadcast_clamp_fusion.1), kind=kCustom, calls=%fused_computation | custom fusion | bytes 98304 | tf_op jit(solution)/shard_map/gather | solution.py:50
  89.9 0.1 compare_select_fusion
  90.0 0.1 subtract_convert_fusion.1
  90.1 38.2 %gather_fusion.1 = f32[8192,17]{1,0:T(8,128)} fusion(f32[17,65536]{0,1:T(8,128)} %bitcast.24, s32[8192]{0:T(1024)S(1)} %broadcast_clamp_fusion), kind=kCustom, calls=%fused_computation.1 | custom fusion | bytes 1146880 | tf_op jit(solution)/shard_map/jit(_take)/gather | solution.py:51
  128.3 9.7 %multiply_bitcast_fusion = f32[17,8192]{0,1:T(8,128)} fusion(f32[8192,17]{1,0:T(8,128)} %gather_fusion.1, f32[8192]{0:T(1024)S(1)} %subtract_convert_fusion.1, pred[8192]{0:T(1024)(128)(4,1)S(1)} %compare_and_fusion), kind=kLoop, calls=%fused_computation.9 | loop fusion | flops 278528 | bytes 1155072 | tf_op jit(solution)/shard_map/mul | solution.py:54
  138.0 0.0 reduce-scatter.3.cloned.1.call-update
  138.0 0.0 reduce-scatter.5.cloned.1.call-start
  138.1 11.8 %gather_fusion.2 = s32[2048]{0:T(1024)S(1)} fusion(s32[8192]{0:T(1024)S(1)} %copy-done, s32[2048]{0:T(1024)S(1)} %broadcast_clamp_fusion.2), kind=kCustom, calls=%fused_computation.2 | custom fusion | bytes 24576 | tf_op jit(solution)/shard_map/gather | solution.py:57
  149.9 0.8 dynamic_slice.6
  150.7 67.0 %reduce-scatter.3.cloned.1.call-done = f32[17,2048]{0,1:T(8,128)} async-done(((f32[17,8192]{0,1:T(8,128)}), f32[17,2048]{0,1:T(8,128)}) %reduce-scatter.3.cloned.1.call-update) | async-done | bytes 139280 | tf_op jit(solution)/shard_map/reduce_scatter | solution.py:54
  217.7 2.6 broadcast_multiply_fusion
  220.3 0.0 reduce-scatter.5.cloned.1.call-update
  220.3 37.1 %reduce-scatter.5.cloned.1.call-done = f32[17,256]{0,1:T(8,128)} async-done(((f32[17,2048]{0,1:T(8,128)}), f32[17,256]{0,1:T(8,128)}) %reduce-scatter.5.cloned.1.call-update) | async-done | bytes 17424 | tf_op jit(solution)/shard_map/reduce_scatter | solution.py:59
  257.4 1.6 copy.15
  259.0 1.0 copy.13
  260.0 1.2 fusion.6
  261.1 39.6 %psum.7 = f32[8,16,17]{2,0,1:T(8,128)S(1)} all-reduce(f32[8,16,17]{2,0,1:T(8,128)S(1)} %fusion.6), channel_id=1, replica_groups=mesh['wide'=8,'quad'=4] {'wide','quad'}, use_global_device_ids=true, to_apply=%region_2.3 | all-reduce | flops 2176 | bytes 17408 | tf_op jit(solution)/shard_map/psum | solution.py:72
  300.8 0.6 copy.16
  (9 shorter events, 0.2 us)
Async XLA Ops:
  7.2 37.1 %copy-start = (s32[8192]{0:T(1024)S(1)}, s32[8192]{0:T(1024)}, u32[]{:S(2)}) copy-start(s32[8192]{0:T(1024)} %param.8) | copy-start | bytes 98308
  7.2 210.5 %reduce-scatter.3.cloned.1.call-start = ((), (), s32[]{:S(2)}) async-start(), calls=%async_computation.2 | async-start | bytes 5242880 | tf_op jit(solution)/shard_map/reduce_scatter | solution.py:54
  7.3 6.4 %copy-start.1 = (s32[65536]{0:T(1024)S(1)}, s32[65536]{0:T(1024)}, u32[]{:S(2)}) copy-start(s32[65536]{0:T(1024)} %param.7) | copy-start | bytes 786436
  138.0 119.4 %reduce-scatter.5.cloned.1.call-start = ((), (), s32[]{:S(2)}) async-start(), calls=%async_computation.3 | async-start | bytes 1179648 | tf_op jit(solution)/shard_map/reduce_scatter | solution.py:59
Sparse Core Ops, SparseCore 0:
  138.2 79.5 reduce-scatter.2
  220.9 36.4 reduce-scatter.4
where the time goes:
time: 309 us; the launch traced here: 308 us
  local copies, waits for them, and re-layouts  124 us (40%)
  waiting for transfers between devices  104 us (34%)
  blocking collectives  39.6 us (13%)
  between operations  14.2 us (5%)
  matrix products  13.6 us (4%)
  other arithmetic  12.7 us (4%)
    reduce_scatter x1, waiting for transfers between devices, shards(): lax.psum_scatter(values * sign[None, :], 'quad', scatter_dimension=1, til...  67 us
    gather x1, local copies, waits for them, and re-layouts, shards(): number = samples[slots]  45.5 us
    psum x1, blocking collectives, shards(): summed = lax.psum(partial_gram, ('wide', 'quad'))  39.6 us
    gather x1, local copies, waits for them, and re-layouts, shards(): values = jnp.take(local, number % rows, axis=1)  38.2 us
    reduce_scatter x1, waiting for transfers between devices, shards(): lax.psum_scatter(shared * (scale * wide_sign)[None, :], 'wide', scatter_d...  37.1 us
    reshape x1, local copies, waits for them, and re-layouts, shards(): local = cube.reshape(width, rows)  18 us
    gather x1, local copies, waits for them, and re-layouts, shards(): outer = samples[mine] // rows // n_quad  11.8 us
    mul x1, other arithmetic, shards(): values * sign[None, :]  9.67 us
  transfers between devices with their start and end apart: 2, of which 2 were waited for; matrix products, arithmetic and copies ran while one was open for 4% of the time, Pallas kernels for 0%

commit v1 on v0

--- a/solution.py
+++ b/solution.py
@@ -69,7 +69,7 @@
     )
     partial_gram = partial_gram * (GROUPS / total_samples)
     owned = GROUPS // n_quad
-    summed = lax.psum(partial_gram, ("wide", "quad"))
+    summed = jnp.sum(lax.all_gather(partial_gram, ("wide", "quad")), axis=0)
     gram = lax.dynamic_slice_in_dim(summed, my_quad * owned, owned, 0)
     return (sketch, gram)
 

time: 309 us -> 357 us (1.16)
  blocking collectives: 39.6 us -> 87.7 us
    all_gather x0 -> x1, blocking collectives: none -> 87.7 us  [shards(): summed = jnp.sum(lax.all_gather(partial_gram, ('wide', 'quad')), axis=0)]
    psum x1 -> x0, blocking collectives: 39.6 us -> none  [shards(): summed = lax.psum(partial_gram, ('wide', 'quad'))]
where the time goes in v1:
time: 357 us
  local copies, waits for them, and re-layouts  124 us (35%)
  waiting for transfers between devices  104 us (29%)
  blocking collectives  87.7 us (25%)
  between operations  14.2 us (4%)
  matrix products  13.6 us (4%)
  other arithmetic  12.8 us (4%)
    all_gather x1, blocking collectives, shards(): summed = jnp.sum(lax.all_gather(partial_gram, ('wide', 'quad')), axis=0)  87.7 us
    reduce_scatter x1, waiting for transfers between devices, shards(): lax.psum_scatter(values * sign[None, :], 'quad', scatter_dimension=1, til...  67 us
    gather x1, local copies, waits for them, and re-layouts, shards(): number = samples[slots]  45.5 us
    gather x1, local copies, waits for them, and re-layouts, shards(): values = jnp.take(local, number % rows, axis=1)  38.2 us
    reduce_scatter x1, waiting for transfers between devices, shards(): lax.psum_scatter(shared * (scale * wide_sign)[None, :], 'wide', scatter_d...  37.1 us
    reshape x1, local copies, waits for them, and re-layouts, shards(): local = cube.reshape(width, rows)  18 us
    gather x1, local copies, waits for them, and re-layouts, shards(): outer = samples[mine] // rows // n_quad  11.8 us
    mul x1, other arithmetic, shards(): values * sign[None, :]  9.67 us
  transfers between devices with their start and end apart: 2, of which 2 were waited for; matrix products, arithmetic and copies ran while one was open for 4% of the time, Pallas kernels for 0%

profile of v1, /device:TPU:0, one launch (start us, length us, event | category | flops | bytes accessed | tf_op | source)
XLA Modules:
  0.0 356.5 jit_solution(13810625368041413566)
XLA Ops:
  7.2 0.0 copy-start
  7.2 0.0 reduce-scatter.3.cloned.1.call-start
  7.2 0.1 compare_select_fusion.1
  7.3 0.0 copy-start.1
  7.4 1.1 concatenate.9
  8.4 5.4 %copy.26 = f32[2,8,256,256]{3,2,1,0:T(8,128)} copy(f32[2,8,256,256]{3,1,2,0:T(8,128)} %bitcast.29) | data formatting | bytes 8388608
  13.8 0.0 copy-done.1
  13.8 0.1 mul.137
  13.9 6.7 %fusion = f32[256,17,256]{2,0,1:T(8,128)S(1)} fusion(f32[1,256,256]{2,1,0:T(8,128)S(1)} %concatenate.9, f32[16,256,256]{2,1,0:T(8,128)} %bitcast.28, f32[256,256]{1,0:T(8,128)S(1)} %mul.137), kind=kOutput, calls=%fused_computation.4 | convolution fusion | flops 3426615296 | bytes 9175040 | tf_op jit(solution)/shard_map/kab,ac->kcb/dot_general | solution.py:40
  20.6 5.7 %fusion.3 = f32[17,256,256]{2,1,0:T(8,128)} fusion(f32[256,17,256]{2,0,1:T(8,128)S(1)} %fusion), kind=kOutput, calls=%fused_computation.7 | convolution fusion | flops 3424387072 | bytes 8912896 | tf_op jit(solution)/shard_map/kcb,bd->kcd/dot_general | solution.py:41
  26.3 18.0 %copy.24 = f32[17,256,256]{0,2,1:T(8,128)} copy(f32[17,256,256]{2,1,0:T(8,128)} %fusion.3) | data formatting | bytes 8912896 | tf_op jit(solution)/shard_map/reshape | solution.py:42
  44.3 0.0 copy-done
  44.3 45.5 %gather_fusion = s32[8192]{0:T(1024)S(1)} fusion(s32[8192]{0:T(1024)S(1)} %copy-done, s32[8192]{0:T(1024)S(1)} %broadcast_clamp_fusion.1), kind=kCustom, calls=%fused_computation | custom fusion | bytes 98304 | tf_op jit(solution)/shard_map/gather | solution.py:50
  89.9 0.1 compare_select_fusion
  90.0 0.1 subtract_convert_fusion.1
  90.1 38.2 %gather_fusion.1 = f32[8192,17]{1,0:T(8,128)} fusion(f32[17,65536]{0,1:T(8,128)} %bitcast.27, s32[8192]{0:T(1024)S(1)} %broadcast_clamp_fusion), kind=kCustom, calls=%fused_computation.1 | custom fusion | bytes 1146880 | tf_op jit(solution)/shard_map/jit(_take)/gather | solution.py:51
  128.3 9.7 %multiply_bitcast_fusion = f32[17,8192]{0,1:T(8,128)} fusion(f32[8192,17]{1,0:T(8,128)} %gather_fusion.1, f32[8192]{0:T(1024)S(1)} %subtract_convert_fusion.1, pred[8192]{0:T(1024)(128)(4,1)S(1)} %compare_and_fusion), kind=kLoop, calls=%fused_computation.9 | loop fusion | flops 278528 | bytes 1155072 | tf_op jit(solution)/shard_map/mul | solution.py:54
  138.0 0.0 reduce-scatter.3.cloned.1.call-update
  138.0 0.0 reduce-scatter.5.cloned.1.call-start
  138.1 11.8 %gather_fusion.2 = s32[2048]{0:T(1024)S(1)} fusion(s32[8192]{0:T(1024)S(1)} %copy-done, s32[2048]{0:T(1024)S(1)} %broadcast_clamp_fusion.2), kind=kCustom, calls=%fused_computation.2 | custom fusion | bytes 24576 | tf_op jit(solution)/shard_map/gather | solution.py:57
  149.9 0.8 dynamic_slice.6
  150.7 67.0 %reduce-scatter.3.cloned.1.call-done = f32[17,2048]{0,1:T(8,128)} async-done(((f32[17,8192]{0,1:T(8,128)}), f32[17,2048]{0,1:T(8,128)}) %reduce-scatter.3.cloned.1.call-update) | async-done | bytes 139280 | tf_op jit(solution)/shard_map/reduce_scatter | solution.py:54
  217.7 2.6 broadcast_multiply_fusion
  220.3 0.0 reduce-scatter.5.cloned.1.call-update
  220.3 37.1 %reduce-scatter.5.cloned.1.call-done = f32[17,256]{0,1:T(8,128)} async-done(((f32[17,2048]{0,1:T(8,128)}), f32[17,256]{0,1:T(8,128)}) %reduce-scatter.5.cloned.1.call-update) | async-done | bytes 17424 | tf_op jit(solution)/shard_map/reduce_scatter | solution.py:59
  257.4 1.6 copy.19
  259.0 1.0 copy.17
  260.0 1.2 fusion.6
  261.1 87.7 %all-gather = f32[256,16,17]{2,0,1:T(8,128)S(1)} all-gather(f32[8,16,17]{2,0,1:T(8,128)S(1)} %fusion.6), channel_id=2, replica_groups=mesh['wide'=8,'quad'=4] {'wide','quad'}, dimensions={0}, use_global_device_ids=true | all-gather | bytes 287232 | tf_op jit(solution)/shard_map/all_gather | solution.py:72
  348.9 0.1 bitcast_reduce_fusion
  349.1 0.6 copy.20
  (9 shorter events, 0.1 us)
Async XLA Ops:
  7.2 37.1 %copy-start = (s32[8192]{0:T(1024)S(1)}, s32[8192]{0:T(1024)}, u32[]{:S(2)}) copy-start(s32[8192]{0:T(1024)} %param.8) | copy-start | bytes 98308
  7.2 210.5 %reduce-scatter.3.cloned.1.call-start = ((), (), s32[]{:S(2)}) async-start(), calls=%async_computation.2 | async-start | bytes 5242880 | tf_op jit(solution)/shard_map/reduce_scatter | solution.py:54
  7.3 6.4 %copy-start.1 = (s32[65536]{0:T(1024)S(1)}, s32[65536]{0:T(1024)}, u32[]{:S(2)}) copy-start(s32[65536]{0:T(1024)} %param.7) | copy-start | bytes 786436
  138.0 119.4 %reduce-scatter.5.cloned.1.call-start = ((), (), s32[]{:S(2)}) async-start(), calls=%async_computation.3 | async-start | bytes 1179648 | tf_op jit(solution)/shard_map/reduce_scatter | solution.py:59
Sparse Core Ops, SparseCore 0:
  138.2 79.5 reduce-scatter.2
  220.9 36.4 reduce-scatter.4
